TPU v7x, 32 devices: a whole 2x2x4 slice. The times are simulated.
32 devices in a mesh: bond: 16 (over z, y, x), op: 2 (over core).
Axes of the slice: x: 2, y: 2, z: 4, core: 2. Of those that a mesh axis runs over, the one named last changes fastest.
Arguments:
- wavefunction: float32 [6, 256, 8192], P(None, None, 'bond'), may hold values from -6 to 6
- left_tiles: bfloat16 [16, 16, 2, 128, 128], P('op', None, None, 'bond'), may hold values from -0.375 to 0.375
- right_tiles: bfloat16 [16, 16, 2, 128, 128], P('op', None, None, 'bond'), may hold values from -0.375 to 0.375
- site_operators: float32 [16, 4, 4], P('op'), may hold values from -1.75 to 1.75
- left_charge: int32 [16], replicated, may hold values from 0 to 7, as said below
- right_charge: int32 [16], replicated, may hold values from 0 to 7, as said below
- channel_charge: int32 [16, 2], replicated, may hold values from -1 to 7, as said below
Outputs:
- sigma_one: float32 [6, 256, 8192], P(None, 'bond', 'op')
- sigma_two: float32 [6, 256, 8192], P(None, 'op', 'bond')
Inputs may be any that keep to these rules, and one draw needn't show every extreme that they name: `left_charge`: each charge labels exactly 2 of the left blocks. `right_charge`: each charge labels exactly 2 of the right blocks. `channel_charge`: column 0 is a left charge shift, each of 0 to 7 used by exactly 2 channels; column 1 is a site charge shift, each of -1, 0 and 1 used by 5 or 6 channels.
All inputs are finite; a program needn't handle non-finite values.
Results may differ from a plain program's by a relative error of at most 0.0057.
Values may be sent and summed in bfloat16 or wider, within the bound.
A program may use at most 128 MiB of HBM per device.

v0:
```python
import functools

import jax
import jax.numpy as jnp
from jax import lax
from jax.experimental import pallas as pl
from jax.experimental.pallas import tpu as pltpu
from jax.sharding import PartitionSpec as P

M = 2048
B = 128
NQ = 8
DP = 4
NB = 16
NPB = 2

site_charge_table = (0, 1, 1, 2)
MESH = pl.DeviceIdType.MESH


def site_masks(site_operators, channel_charge):
    site_charge = jnp.array(site_charge_table, dtype=jnp.int32)
    charge_step = site_charge[:, None] - site_charge[None, :]
    allowed = (charge_step[None, :, :] - channel_charge[:, 1][:, None, None]) % NQ == 0
    return jnp.where(allowed, site_operators, jnp.zeros_like(site_operators))


def spread_kernel(half, ops, colours, first, *refs):
    if first:
        x_ref, y_ref, g_ref = refs[:3]
        z_ref = None
        scratch = refs[3:]
    else:
        x_ref, y_ref, g_ref, z_ref = refs[:4]
        scratch = refs[4:]
    own_sem, psend, precv, send_sem, recv_sem, fsend, frecv = scratch
    bond = lax.axis_index("bond")
    o = lax.axis_index("op")
    i = lax.rem(bond, half)
    part = bond // half
    base = bond - i
    partner = i + half * (1 - part)
    bits = half.bit_length() - 1
    streams = 2 if first else 1

    def place(mask):
        at = i
        for t in range(bits):
            if mask >> t & 1:
                at = at + (1 << t) * (1 - 2 * lax.rem(i // (1 << t), 2))
        return at

    def to(bond_index, op_index):
        return {"bond": bond_index, "op": op_index}

    barrier = pltpu.get_barrier_semaphore()
    for t in range(bits):
        pl.semaphore_signal(
            barrier, inc=1, device_id=to(base + place(1 << t), o), device_id_type=MESH
        )
    pl.semaphore_signal(barrier, inc=1, device_id=to(partner, o), device_id_type=MESH)
    for e in range(1, ops):
        pl.semaphore_signal(
            barrier, inc=1, device_id=to(bond, lax.rem(o + e, ops)), device_id_type=MESH
        )
    pl.semaphore_wait(barrier, bits + ops)

    index = (part, 1 - part) if first else (0,)
    exchange = []
    for c in range(colours if first else 1):
        exchange.append(pltpu.make_async_remote_copy(
            src_ref=y_ref.at[c] if first else y_ref,
            dst_ref=g_ref.at[i, o, part, c] if first else z_ref,
            send_sem=psend.at[c], recv_sem=precv.at[c],
            device_id=to(partner, o), device_id_type=MESH,
        ))
        exchange[-1].start()

    copies = {}
    forwards = []
    ready = set()

    def block(s, c, mask):
        if s == 0 and mask == 0:
            return x_ref.at[c]
        return g_ref.at[place(mask), o, index[s], c]

    def ensure(s, c, mask):
        if (s, c, mask) in ready:
            return
        ready.add((s, c, mask))
        if mask:
            copies[s, c, mask].wait_recv()
        elif s == 1:
            exchange[c].wait_recv()
        for e in range(1, ops):
            copy = pltpu.make_async_remote_copy(
                src_ref=block(s, c, mask), dst_ref=g_ref.at[place(mask), o, index[s], c],
                send_sem=fsend.at[s, c, mask, e], recv_sem=frecv.at[s, c, mask, e],
                device_id=to(bond, lax.rem(o + e, ops)), device_id_type=MESH,
            )
            copy.start()
            forwards.append(copy)

    own = pltpu.make_async_copy(x_ref, g_ref.at[i, o, index[0]], own_sem)
    own.start()
    for s in range(streams):
        reached = [[0] for c in range(colours)]
        for step in range(bits):
            for at in range(max(len(r) for r in reached)):
                for c in range(colours):
                    mask = reached[c][at]
                    bit = 1 << (c + step) % bits
                    ensure(s, c, mask)
                    copy = pltpu.make_async_remote_copy(
                        src_ref=block(s, c, mask), dst_ref=g_ref.at[place(mask), o, index[s], c],
                        send_sem=send_sem.at[s, c, mask | bit], recv_sem=recv_sem.at[s, c, mask | bit],
                        device_id=to(base + place(bit), o), device_id_type=MESH,
                    )
                    copy.start()
                    copies[s, c, mask | bit] = copy
            for c in range(colours):
                bit = 1 << (c + step) % bits
                reached[c] = reached[c] + [mask | bit for mask in reached[c]]
    for s in range(streams):
        for mask in range(half):
            for c in range(colours):
                ensure(s, c, mask)
    own.wait()
    for copy in copies.values():
        copy.wait_send()
    for copy in exchange:
        copy.wait_send()
        if not first:
            copy.wait_recv()
    for copy in forwards:
        copy.wait()


def spread(x, y, half, ops, first):
    colours = x.shape[0]
    streams = 2 if first else 1
    shapes = [jax.ShapeDtypeStruct((half, ops, streams) + x.shape, x.dtype)]
    if not first:
        shapes.append(jax.ShapeDtypeStruct(y.shape, y.dtype))
    size = x.size * half * ops * streams * 2
    return pl.pallas_call(
        functools.partial(spread_kernel, half, ops, colours, first),
        out_shape=shapes,
        in_specs=[pl.BlockSpec(memory_space=pltpu.VMEM)] * 2,
        out_specs=[pl.BlockSpec(memory_space=pl.ANY)] * len(shapes),
        scratch_shapes=[
            pltpu.SemaphoreType.DMA,
            pltpu.SemaphoreType.DMA((colours,)),
            pltpu.SemaphoreType.DMA((colours,)),
            pltpu.SemaphoreType.DMA((streams, colours, half)),
            pltpu.SemaphoreType.DMA((streams, colours, half)),
            pltpu.SemaphoreType.DMA((streams, colours, half, ops)),
            pltpu.SemaphoreType.DMA((streams, colours, half, ops)),
        ],
        compiler_params=pltpu.CompilerParams(
            collective_id=1 if first else 2, has_side_effects=True
        ),
        cost_estimate=pl.CostEstimate(flops=0, bytes_accessed=16 * size, transcendentals=0),
        name="spread_first" if first else "spread_second",
    )(x, y)


def apply_kernel(
    channels, rows, roots, site_charges, load,
    order_ref, shift_ref, site_ref, psi_ref, left_ref, right_ref, out_ref, mixed
):
    @pl.loop(0, NQ)
    def _(g):
        for n in range(NPB):
            r = order_ref[g * NPB + n]
            terms = []
            for q in range(DP):
                h = lax.rem(2 * NQ - site_charges[q] - g, NQ)
                terms.append(
                    jnp.dot(left_ref[h], load(psi_ref, q * NB + r), preferred_element_type=jnp.float32)
                )
            for c in range(channels):
                for p in range(DP):
                    total = site_ref[(c * DP + p) * DP] * terms[0][c * rows:(c + 1) * rows]
                    for q in range(1, DP):
                        total += site_ref[(c * DP + p) * DP + q] * terms[q][c * rows:(c + 1) * rows]
                    total = total.astype(jnp.bfloat16)
                    for k in range(roots):
                        at = (p * roots + k) * rows
                        mixed[c, g, at:at + rows, n * B:(n + 1) * B] = total[:, k * B:(k + 1) * B]

    @pl.loop(0, NQ)
    def _(g):
        total = None
        for c in range(channels):
            source = lax.rem(g + shift_ref[c], NQ)
            term = lax.dot_general(
                mixed[c, source], right_ref[c, g], (((1,), (1,)), ((), ())),
                preferred_element_type=jnp.float32,
            )
            total = term if total is None else total + term
        for m in range(NPB):
            out_ref[order_ref[g * NPB + m]] = total[:, m * B:(m + 1) * B]


def apply_all(order, shift, site, psi, left, right, rows, roots, load):
    channels = right.shape[0]
    height = DP * roots * rows
    smem = pl.BlockSpec(memory_space=pltpu.SMEM)
    vmem = pl.BlockSpec(memory_space=pltpu.VMEM)
    return pl.pallas_call(
        functools.partial(apply_kernel, channels, rows, roots, site_charge_table, load),
        out_shape=jax.ShapeDtypeStruct((NB, height, B), jnp.float32),
        in_specs=[smem, smem, smem, vmem, vmem, vmem],
        out_specs=vmem,
        scratch_shapes=[pltpu.VMEM((channels, NQ, height, NPB * B), jnp.bfloat16)],
        compiler_params=pltpu.CompilerParams(vmem_limit_bytes=58 * 1024 * 1024),
        name="apply_all",
    )(order, shift, site, psi, left, right)


def local(
    wavefunction, left_tiles, right_tiles, site_operators, left_charge, right_charge, channel_charge
):
    bonds = lax.axis_size("bond")
    ops = lax.axis_size("op")
    bond = lax.axis_index("bond")
    op = lax.axis_index("op")
    roots, sector_rows, strip = wavefunction.shape
    channels = site_operators.shape[0]
    half = bonds // 2
    part = bond // half
    some = roots // 2
    chunk = left_tiles.shape[3]
    band = 2 * chunk
    rows = NPB * band
    held = -(-rows // 16) * 16
    width = min(strip, B)
    groups = strip // width
    own_charge = lax.dynamic_slice_in_dim(channel_charge, op * channels, channels, 0)
    left_order = jnp.argsort(left_charge, stable=True).astype(jnp.int32)
    right_order = jnp.argsort(right_charge, stable=True).astype(jnp.int32)
    shift = (own_charge[:, 0] + own_charge[:, 1]) % NQ
    site = site_masks(site_operators, own_charge).reshape(-1)

    right = right_tiles[:, right_order].transpose(0, 1, 3, 2, 4).reshape(
        channels, NB, chunk, NPB * B
    )
    right = lax.all_gather(right, "bond", axis=2, tiled=True).reshape(
        channels, NQ, NPB * B, NPB * B
    )

    even = [(b, b // 2 + (b % 2) * half) for b in range(bonds)]
    odd = [(b, b // 2 + (1 - b % 2) * half) for b in range(bonds)]
    one = lax.ppermute(left_tiles, "bond", even)
    two = lax.ppermute(left_tiles, "bond", odd)
    low = jnp.where(part == 0, one, two)
    high = jnp.where(part == 0, two, one)
    left = jnp.concatenate([low, high], axis=3)
    left_slots = ((jnp.arange(NQ)[:, None] + own_charge[None, :, 0]) % NQ)[:, :, None] * NPB + jnp.arange(NPB)
    left = left[jnp.arange(channels)[None, :, None], left_order[left_slots]]
    left = left.transpose(0, 1, 2, 4, 3, 5).reshape(NQ, channels, rows, NPB * B)
    left = jnp.pad(left, ((0, 0), (0, 0), (0, held - rows), (0, 0)))
    left = left.reshape(NQ, channels * held, NPB * B)

    share = sector_rows // ops
    psi = lax.dynamic_slice_in_dim(wavefunction, op * share, share, 1).astype(jnp.bfloat16)
    psi = psi.reshape(2, some, share, groups, width).transpose(0, 1, 3, 2, 4)
    kept = lax.dynamic_index_in_dim(psi, part, 0, keepdims=False)
    other = lax.dynamic_index_in_dim(psi, 1 - part, 0, keepdims=False)
    (psi,) = spread(kept, other, half, ops, True)

    def load_whole(ref, block):
        return ref[block]

    def load_first(ref, block):
        owner = block // groups
        t, j, at = owner // half, lax.rem(owner, half), lax.rem(block, groups)
        return jnp.concatenate(
            [jnp.concatenate([ref[j, o, t, k, at] for o in range(ops)], 0) for k in range(some)], 1
        )

    load = load_first
    if width < B:
        psi = psi.reshape(half, ops, 2, some, share, strip).transpose(2, 0, 5, 1, 4, 3)
        psi = psi.reshape(DP * NB, B, sector_rows, some).transpose(0, 2, 3, 1)
        psi = psi.reshape(DP * NB, sector_rows, some * B)
        load = load_whole
    elif share % 16:
        psi = psi.transpose(2, 0, 4, 1, 5, 3, 6).reshape(DP * NB, sector_rows, some * B)
        load = load_whole

    def unpack(result):
        result = result.reshape(NB, DP, some, held, B)[:, :, :, :rows]
        return result.reshape(NB, DP, some, NPB, band, B)

    def summed_share(parts, axis):
        size = parts.shape[axis] // ops
        total = lax.dynamic_slice_in_dim(parts, op * size, size, axis)
        for e in range(1, ops):
            to = (op + e) % ops
            sent = lax.dynamic_slice_in_dim(parts, to * size, size, axis)
            total += lax.ppermute(sent, "op", [(o, (o + e) % ops) for o in range(ops)])
        return total

    first = unpack(apply_all(right_order, shift, site, psi, left, right, held, some, load))
    turned = (DP * NB, some, NPB, band, B)
    if DP % ops == 0:
        first = summed_share(first, 1).transpose(1, 0, 2, 3, 4, 5)
        first = first.reshape((DP * NB // ops,) + turned[1:])
    else:
        first = summed_share(first.transpose(1, 0, 2, 3, 4, 5).reshape(turned), 0)
    blocks = first.shape[0]

    mine = lax.dynamic_index_in_dim(first, part, 2, keepdims=False)
    theirs = lax.dynamic_index_in_dim(first, 1 - part, 2, keepdims=False)
    again = first.astype(jnp.bfloat16).transpose(1, 0, 2, 3, 4)
    again, back = spread(again, theirs.astype(jnp.bfloat16), half, ops, False)
    back = back.astype(jnp.float32)
    both = jnp.stack([jnp.where(part == 0, mine, back), jnp.where(part == 0, back, mine)])
    sigma_one = both.transpose(0, 2, 3, 1, 4).reshape(roots, band, blocks * B)

    def load_second(ref, block):
        o, at = block // blocks, lax.rem(block, blocks)
        return jnp.concatenate(
            [
                jnp.concatenate([ref[j, o, 0, k, at, m] for m in range(NPB) for j in range(half)], 0)
                for k in range(some)
            ], 1,
        )

    load = load_second
    if band % 16:
        again = again[:, :, 0].transpose(1, 3, 4, 0, 5, 2, 6)
        again = again.reshape(DP * NB, sector_rows, some * B)
        load = load_whole
    second = unpack(apply_all(right_order, shift, site, again, left, right, held, some, load))
    if ops == NPB:
        second = summed_share(second, 3)
    else:
        second = lax.psum(second, "op")
    tiles = second.shape[3]
    second = second.astype(jnp.bfloat16).transpose(2, 3, 4, 1, 0, 5)
    second = second.reshape(some, tiles * band, bonds, strip).transpose(2, 0, 1, 3)
    second = lax.all_to_all(second, "bond", split_axis=0, concat_axis=0, tiled=True)
    second = second.reshape(2, half, some, tiles, band, strip).transpose(0, 2, 3, 1, 4, 5)
    second = second.reshape(roots, tiles * B, strip).astype(jnp.float32)
    if ops != NPB:
        second = lax.dynamic_slice_in_dim(second, op * share, share, 1)
    return (sigma_one, second)


def solution(mesh):
    return jax.shard_map(
        local,
        mesh=mesh,
        in_specs=(
            P(None, None, "bond"),
            P("op", None, None, "bond", None),
            P("op", None, None, "bond", None),
            P("op", None, None),
            P(),
            P(),
            P(),
        ),
        out_specs=(P(None, "bond", "op"), P(None, "op", "bond")),
        check_vma=False,
    )
```

profile of v0, /device:TPU:14, one launch (start us, length us, event | category | flops | bytes accessed | tf_op | source)
XLA Modules:
  0.0 351.5 jit_solution(10204228203852498713)
XLA Ops:
  7.3 2.0 sort.31
  9.3 2.5 gather_fusion.2
  11.8 1.9 copy_bitcast_fusion.1
  13.7 3.5 collective-permute-start
  17.2 1.5 collective-permute-start.1
  20.7 1.5 copy.55
  24.4 1.3 sort.32
  25.7 1.2 gather_fusion
  27.2 86.1 %spread_first.1.psi_ref = bf16[8,2,2,3,4,128,128]{6,5,4,3,2,1,0:T(8,128)(2,1)} custom-call(bf16[3,4,128,128]{3,2,1,0:T(8,128)(2,1)} %bitcast.76, bf16[3,4,128,128]{3,2,1,0:T(8,128)(2,1)} %bitcast.77), custom_call_target="tpu_custom_call" | custom-call | bytes 201326592 | tf_op jit(solution)/shard_map/spread_first/pallas_call | solution.py:147
  113.9 1.3 broadcast_select_fusion.1
  116.3 1.2 copy.70
  117.5 1.5 reshape.131.left_ref
  119.0 66.3 %all-gather.2.cloned.1.call-done = bf16[8,16,128,256]{3,2,1,0:T(8,128)(2,1)} async-done(((bf16[8,16,8,256]{3,2,1,0:T(8,128)(2,1)}), bf16[8,16,128,256]{3,2,1,0:T(8,128)(2,1)}) %all-gather.2.cloned.1.call-update) | async-done | bytes 8388624 | tf_op jit(solution)/shard_map/all_gather | solution.py:250
  185.3 24.8 %apply_all.2 = f32[16,384,128]{2,1,0:T(8,128)} custom-call(s32[16]{0:T(128)} %copy-done.5, s32[8]{0:T(128)} %and_select_fusion.shift_ref, f32[128]{0:T(128)} %reshape.129.site_ref, bf16[8,2,2,3,4,128,128]{6,5,4,3,2,1,0:T(8,128)(2,1)} %spread_first.1.psi_ref, bf16[8,256,256]{2,1,0:T(8,128)(2,1)} %reshape.131.left_ref, bf16[8,8,256,256]{3,2,1,0:T(8,128)(2,1)} %bitcast.65), custom_call_target="tpu_custom_call" | custom-call | tf_op jit(solution)/shard_map/apply_all/pallas_call | solution.py:212
  210.1 2.4 constant_dynamic-slice_fusion.3
  212.5 1.3 copy.59
  213.8 3.6 %collective-permute-done.2 = f32[16,2,3,2,16,128]{5,4,2,0,1,3:T(8,128)S(1)} collective-permute-done((f32[16,2,3,2,16,128]{5,4,2,0,1,3:T(8,128)}, f32[16,2,3,2,16,128]{5,4,2,0,1,3:T(8,128)S(1)}, u32[]{:S(2)}, u32[]{:S(2)}) %collective-permute-start.2) | collective-permute-done | bytes 1572896 | tf_op jit(solution)/shard_map/ppermute | solution.py:304
  217.4 1.1 copy-done.2
  218.6 1.6 copy_add_fusion.1
  221.1 1.0 copy.49.refs_0_
  222.1 57.4 %spread_second.1 = (bf16[8,2,1,3,32,2,16,128]{7,6,5,4,3,2,1,0:T(8,128)(2,1)}, bf16[32,3,16,128]{3,2,1,0:T(8,128)(2,1)}) custom-call(bf16[3,32,2,16,128]{4,3,2,1,0:T(8,128)(2,1)} %copy.49.refs_0_, bf16[32,3,16,128]{3,2,1,0:T(8,128)(2,1)} %fusion.4.refs_1_), custom_call_target="tpu_custom_call" | custom-call | bytes 201326592 | tf_op jit(solution)/shard_map/spread_second/pallas_call | solution.py:147
  279.5 24.8 %apply_all.3 = f32[16,384,128]{2,1,0:T(8,128)} custom-call(s32[16]{0:T(128)} %copy-done.5, s32[8]{0:T(128)} %and_select_fusion.shift_ref, f32[128]{0:T(128)} %reshape.129.site_ref, bf16[8,2,1,3,32,2,16,128]{7,6,5,4,3,2,1,0:T(8,128)(2,1)} %get-tuple-element.9.psi_ref, bf16[8,256,256]{2,1,0:T(8,128)(2,1)} %reshape.131.left_ref, bf16[8,8,256,256]{3,2,1,0:T(8,128)(2,1)} %bitcast.66), custom_call_target="tpu_custom_call" | custom-call | tf_op jit(solution)/shard_map/apply_all/pallas_call | solution.py:212
  304.3 2.3 constant_dynamic-slice_fusion.1
  308.0 3.0 collective-permute-done.3
  311.0 1.9 fusion.3
  312.9 1.6 reshape.136
  314.4 1.3 copy.53
  315.8 6.8 %all-to-all-start = ((bf16[16,3,16,512]{3,2,1,0:T(8,128)(2,1)}), bf16[16,3,16,512]{3,2,1,0:T(8,128)(2,1)}, u32[]{:S(2)}, u32[]{:S(2)}) async-start(bf16[16,3,16,512]{3,2,1,0:T(8,128)(2,1)} %copy.53), calls=%async_computation | async-start | bytes 1572864 | tf_op jit(solution)/shard_map/all_to_all | solution.py:346
  323.3 1.4 reshape.135
  324.7 17.2 %all-to-all-done = bf16[16,3,16,512]{3,2,1,0:T(8,128)(2,1)} async-done(((bf16[16,3,16,512]{3,2,1,0:T(8,128)(2,1)}), bf16[16,3,16,512]{3,2,1,0:T(8,128)(2,1)}, u32[]{:S(2)}, u32[]{:S(2)}) %all-to-all-start) | async-done | bytes 786464 | tf_op jit(solution)/shard_map/all_to_all | solution.py:346
  341.9 1.5 convert_bitcast_fusion
  343.4 1.3 copy.54
  (55 shorter events, 9.2 us)
Async XLA Ops:
  7.2 12.5 %copy-start = (f32[6,256,512]{2,1,0:T(8,128)S(1)}, f32[6,256,512]{2,1,0:T(8,128)}, u32[]{:S(2)}) copy-start(f32[6,256,512]{2,1,0:T(8,128)} %param.8) | copy-start | bytes 9437188
  7.2 11.6 %copy-start.7 = (s32[4]{0:T(128)S(1)}, s32[4]{0:T(128)}, u32[]{:S(2)}) copy-start(s32[4]{0:T(128)} %constant.104) | copy-start | bytes 52
  7.2 11.6 %copy-start.8 = (s32[4]{0:T(128)S(1)}, s32[4]{0:T(128)}, u32[]{:S(2)}) copy-start(s32[4]{0:T(128)} %constant.101.clone) | copy-start | bytes 52
  7.2 11.5 %copy-start.6 = (s32[16,2]{0,1:T(2,128)S(1)}, s32[16,2]{0,1:T(2,128)}, u32[]{:S(2)}) copy-start(s32[16,2]{0,1:T(2,128)} %param.14) | copy-start | bytes 388
  7.2 11.6 %copy-start.4 = (f32[8,4,4]{0,2,1:T(4,128)S(1)}, f32[8,4,4]{0,2,1:T(4,128)}, u32[]{:S(2)}) copy-start(f32[8,4,4]{0,2,1:T(4,128)} %param.11) | copy-start | bytes 1540
  7.2 178.0 %all-gather.2.cloned.1.call-start = ((), (), s32[]{:S(2)}) async-start(), calls=%async_computation.1 | async-start | bytes 8912896 | tf_op jit(solution)/shard_map/all_gather | solution.py:250
  9.3 11.3 %copy-start.5 = (s32[16]{0:T(128)}, s32[16]{0:T(128)S(1)}, u32[]{:S(2)}) copy-start(s32[16]{0:T(128)S(1)} %get-tuple-element.6.order_ref) | copy-start | bytes 196
  13.7 100.2 %collective-permute-start = (bf16[8,16,2,8,128]{4,3,2,1,0:T(8,128)(2,1)}, bf16[8,16,2,8,128]{4,3,2,1,0:T(8,128)(2,1)}, u32[]{:S(2)}, u32[]{:S(2)}) collective-permute-start(bf16[8,16,2,8,128]{4,3,2,1,0:T(8,128)(2,1)} %param.9), channel_id=1, source_target_pairs={{0,0},{2,16},{4,2},{6,18},{8,4},{10,20},{12,6},{14,22},{16,8},{18,... | collective-permute-start | bytes 1572872 | tf_op jit(solution)/shard_map/ppermute | solution.py:256
  17.2 96.7 %collective-permute-start.1 = (bf16[8,16,2,8,128]{4,3,2,1,0:T(8,128)(2,1)}, bf16[8,16,2,8,128]{4,3,2,1,0:T(8,128)(2,1)}, u32[]{:S(2)}, u32[]{:S(2)}) collective-permute-start(bf16[8,16,2,8,128]{4,3,2,1,0:T(8,128)(2,1)} %param.9), channel_id=1, source_target_pairs={{0,16},{2,0},{4,18},{6,2},{8,20},{10,4},{12,22},{14,6},{16,24},{18... | collective-permute-start | bytes 1572872 | tf_op jit(solution)/shard_map/ppermute | solution.py:257
  22.2 2.2 copy-start.9
  213.8 3.6 %collective-permute-start.2 = (f32[16,2,3,2,16,128]{5,4,2,0,1,3:T(8,128)}, f32[16,2,3,2,16,128]{5,4,2,0,1,3:T(8,128)S(1)}, u32[]{:S(2)}, u32[]{:S(2)}) collective-permute-start(f32[16,2,3,2,16,128]{5,4,2,0,1,3:T(8,128)} %copy.59), channel_id=1, source_target_pairs={{0,1},{1,0},{2,3},{3,2},{4,5},{5,4},{6,7},{7,6},{8,9},{9,8},{10,11... | collective-permute-start | bytes 4718600 | tf_op jit(solution)/shard_map/ppermute | solution.py:304
  217.4 1.1 copy-start.2
  307.5 3.5 collective-permute-start.3
  314.4 8.1 %copy-start.3 = (bf16[32,3,16,128]{3,2,1,0:T(8,128)(2,1)S(1)}, bf16[32,3,16,128]{3,2,1,0:T(8,128)(2,1)}, u32[]{:S(2)}) copy-start(bf16[32,3,16,128]{3,2,1,0:T(8,128)(2,1)} %get-tuple-element.8) | copy-start | bytes 1179652
  315.8 26.1 %all-to-all-start = ((bf16[16,3,16,512]{3,2,1,0:T(8,128)(2,1)}), bf16[16,3,16,512]{3,2,1,0:T(8,128)(2,1)}, u32[]{:S(2)}, u32[]{:S(2)}) async-start(bf16[16,3,16,512]{3,2,1,0:T(8,128)(2,1)} %copy.53), calls=%async_computation | async-start | bytes 1572864 | tf_op jit(solution)/shard_map/all_to_all | solution.py:346
  341.9 2.8 copy-start.1
Sparse Core Ops, SparseCore 0:
  13.8 171.3 all-gather.1
where the time goes:
time: 354 us; the launch traced here: 352 us
  Pallas kernels  193 us (55%)
  waiting for transfers between devices  90.1 us (25%)
  local copies, waits for them, and re-layouts  30.8 us (9%)
  between operations  14.3 us (4%)
  starting transfers between devices  12.2 us (3%)
  other arithmetic  10.9 us (3%)
    pallas_call x2, Pallas kernels, spread(): pl.pallas_call(functools.partial(spread_kernel, half, ops, colours, first...  144 us
    all_gather x1, waiting for transfers between devices, local(): lax.all_gather(right, 'bond', axis=2, tiled=True)  66.3 us
    pallas_call x2, Pallas kernels, apply_all(): pl.pallas_call(functools.partial(apply_kernel, channels, rows, roots, sit...  49.6 us
    all_to_all x1, waiting for transfers between devices, local(): lax.all_to_all(second, 'bond', split_axis=0, concat_axis=0, tiled=True)  17.2 us
  transfers between devices with their start and end apart: 6, of which 4 were waited for; matrix products, arithmetic and copies ran while one was open for 5% of the time, Pallas kernels for 25%

commit v1 on v0

--- a/solution.py
+++ b/solution.py
@@ -220,6 +220,497 @@
     )(order, shift, site, psi, left, right)
 
 
+def whole_kernel(
+    half, ops, some, channels, site_charges,
+    order_ref, rank_ref, left_order_ref, shift_ref, left_shift_ref, site_ref,
+    wave_ref, lt_ref, rt_ref, one_ref, two_ref,
+    psi, gathered, right, left, left_raw, mixed, part_sum, got_first, got_second, stage, away,
+    swap, sorted_out, ready, landed,
+    stage_sem, psend, precv, send_sem, recv_sem, fsend, frecv,
+    rpsend, rprecv, rsend, rrecv, lsend, lrecv, lown, osend, orecv, osend2, orecv2,
+    wsend, wrecv, asend, arecv, free_sem,
+):
+    bond = lax.axis_index("bond")
+    o = lax.axis_index("op")
+    bonds = 2 * half
+    i = lax.rem(bond, half)
+    part = bond // half
+    base = bond - i
+    partner = i + half * (1 - part)
+    bits = half.bit_length() - 1
+    rows = left.shape[1] // channels
+    sub = rows // NPB
+    fine = lt_ref.shape[3]
+    streams = 2
+    other = lax.rem(o + 1, ops)
+
+    def place(mask):
+        at = i
+        for t in range(bits):
+            if mask >> t & 1:
+                at = at + (1 << t) * (1 - 2 * lax.rem(i // (1 << t), 2))
+        return at
+
+    def turn(x):
+        return lax.rem(2 * x, half) + (2 * x) // half
+
+    def to(bond_index, op_index):
+        return {"bond": bond_index, "op": op_index}
+
+    def remote(src, dst, send, recv, bond_index, op_index):
+        return pltpu.make_async_remote_copy(
+            src_ref=src, dst_ref=dst, send_sem=send, recv_sem=recv,
+            device_id=to(bond_index, op_index), device_id_type=MESH,
+        )
+
+    barrier = pltpu.get_barrier_semaphore()
+    for e in range(1, bonds):
+        pl.semaphore_signal(
+            barrier, inc=1, device_id=to(lax.rem(bond + e, bonds), o), device_id_type=MESH
+        )
+    pl.semaphore_signal(barrier, inc=1, device_id=to(bond, other), device_id_type=MESH)
+
+    share = stage.shape[1]
+    groups = stage.shape[2] // B
+    load = pltpu.make_async_copy(wave_ref.at[:, pl.ds(o * share, share), :], stage, stage_sem)
+    load.start()
+    load.wait()
+    tiles = share // sub
+    for k in range(some):
+        for at in range(groups):
+            for t in range(tiles):
+                psi[i, o, k, part, at * tiles + t] = stage[
+                    part * some + k, t * sub:(t + 1) * sub, at * B:(at + 1) * B
+                ].astype(jnp.bfloat16)
+                away[k, at * tiles + t] = stage[
+                    (1 - part) * some + k, t * sub:(t + 1) * sub, at * B:(at + 1) * B
+                ].astype(jnp.bfloat16)
+    pl.semaphore_wait(barrier, bonds)
+
+    def spread(index, exchange):
+        colours = some
+        copies, forwards, ready_set = {}, [], set()
+
+        def slot(s, c, mask):
+            return psi.at[place(mask), o, c, index[s]]
+
+        def ensure(s, c, mask):
+            if (s, c, mask) in ready_set:
+                return
+            ready_set.add((s, c, mask))
+            if mask:
+                copies[s, c, mask].wait_recv()
+            elif s == 1 and exchange:
+                exchange[c].wait_recv()
+            copy = remote(slot(s, c, mask), slot(s, c, mask), fsend.at[s, c, mask],
+                          frecv.at[s, c, mask], bond, other)
+            copy.start()
+            forwards.append(copy)
+
+        reached = [[[0] for c in range(colours)] for s in range(streams)]
+
+        def step(s, n):
+            for at in range(1 << n):
+                for c in range(colours):
+                    mask = reached[s][c][at]
+                    bit = 1 << (c + n) % bits
+                    ensure(s, c, mask)
+                    copy = remote(slot(s, c, mask), slot(s, c, mask), send_sem.at[s, c, mask | bit],
+                                  recv_sem.at[s, c, mask | bit], base + place(bit), o)
+                    copy.start()
+                    copies[s, c, mask | bit] = copy
+            for c in range(colours):
+                bit = 1 << (c + n) % bits
+                reached[s][c] = reached[s][c] + [mask | bit for mask in reached[s][c]]
+
+        def finish():
+            for s in range(streams):
+                for mask in range(half):
+                    for c in range(colours):
+                        ensure(s, c, mask)
+            for copy in copies.values():
+                copy.wait_send()
+            for copy in exchange:
+                copy.wait_send()
+            for copy in forwards:
+                copy.wait()
+
+        return step, finish
+
+    exchange = []
+    for c in range(some):
+        exchange.append(remote(away.at[c], psi.at[i, o, c, part], psend.at[c], precv.at[c], partner, o))
+        exchange[-1].start()
+    psi_step, psi_finish = spread((part, 1 - part), exchange)
+    psi_step(0, 0)
+
+    @pl.loop(0, channels)
+    def _(c):
+        for g in range(NQ):
+            bands = []
+            for m in range(NPB):
+                r = order_ref[g * NPB + m]
+                bands.append(jnp.concatenate(
+                    [rt_ref[c, r, n].astype(jnp.float32) for n in range(NPB)], 1))
+            gathered[bond, c, g] = jnp.concatenate(bands, 0).astype(jnp.bfloat16)
+
+    last = bits - 1
+    orders = [(last, 0, 1), (last, 1, 0), (0, last, 1), (1, last, 0)]
+    paints = len(orders)
+    wide = channels // paints
+
+    def tile(slot, c):
+        return gathered.at[slot, pl.ds(c * wide, wide)]
+
+    right_exchange = []
+    for c in range(paints):
+        right_exchange.append(remote(tile(bond, c), tile(bond, c), rpsend.at[c], rprecv.at[c], partner, o))
+    right_copies, right_ready = {}, set()
+
+    def right_ensure(s, c, mask):
+        if (s, c, mask) in right_ready:
+            return
+        right_ready.add((s, c, mask))
+        if mask:
+            right_copies[s, c, mask].wait_recv()
+        elif s == 1:
+            right_exchange[c].wait_recv()
+
+    right_reached = [[[0] for c in range(paints)] for s in range(streams)]
+
+    def right_step(s, n):
+        start = base if s == 0 else half - base
+        for at in range(1 << n):
+            for c in range(paints):
+                mask = right_reached[s][c][at]
+                bit = 1 << orders[c][n]
+                right_ensure(s, c, mask)
+                here = tile(start + place(mask), c)
+                copy = remote(here, here, rsend.at[s, c, mask | bit], rrecv.at[s, c, mask | bit],
+                              base + place(bit), o)
+                copy.start()
+                right_copies[s, c, mask | bit] = copy
+        for c in range(paints):
+            bit = 1 << orders[c][n]
+            right_reached[s][c] = right_reached[s][c] + [mask | bit for mask in right_reached[s][c]]
+
+    for copy in right_exchange:
+        copy.start()
+    parity = lax.rem(bond, 2)
+    left_targets = []
+    for h in range(2):
+        target = h * half + turn(bond // 2)
+        left_targets.append((target, remote(
+            lt_ref, left_raw.at[parity], lsend.at[h], lrecv.at[parity], target, o)))
+    own_left = pltpu.make_async_copy(lt_ref, left_raw.at[parity], lown)
+    for target, copy in left_targets:
+        @pl.when(target != bond)
+        def _():
+            copy.start()
+
+        @pl.when(target == bond)
+        def _():
+            own_left.start()
+
+    right_step(0, 0)
+    psi_step(0, 1)
+    psi_step(0, 2)
+    right_step(0, 1)
+    psi_step(1, 0)
+    psi_step(1, 1)
+    psi_step(1, 2)
+    right_step(0, 2)
+    right_step(1, 0)
+    right_step(1, 1)
+
+    band = i // 2 + lax.rem(i, 2) * (half // 2)
+    for t in range(2):
+        source = 2 * band + t
+
+        @pl.when(source != bond)
+        def _():
+            remote(lt_ref, left_raw.at[t], lsend.at[0], lrecv.at[t], source, o).wait_recv()
+
+        @pl.when(source == bond)
+        def _():
+            own_left.wait()
+
+    @pl.loop(0, NQ)
+    def _(h):
+        for c in range(channels):
+            slot = lax.rem(h + left_shift_ref[c], NQ)
+            for m in range(NPB):
+                r = left_order_ref[slot * NPB + m]
+                pieces = []
+                for t in range(2):
+                    pieces.append(jnp.concatenate(
+                        [left_raw[t, c, r, n].astype(jnp.float32) for n in range(NPB)], 1))
+                at = c * rows + m * sub
+                left[h, at:at + sub] = jnp.concatenate(pieces, 0).astype(jnp.bfloat16)
+
+    right_step(1, 2)
+    psi_finish()
+
+    def left_dots(fetch):
+        @pl.loop(0, NQ)
+        def _(g):
+            for n in range(NPB):
+                terms = []
+                for q in range(DP):
+                    h = lax.rem(2 * NQ - site_charges[q] - g, NQ)
+                    terms.append(
+                        jnp.dot(left[h], fetch(q, g, n), preferred_element_type=jnp.float32)
+                    )
+                for c in range(channels):
+                    for p in range(DP):
+                        total = site_ref[(c * DP + p) * DP] * terms[0][c * rows:(c + 1) * rows]
+                        for q in range(1, DP):
+                            total += site_ref[(c * DP + p) * DP + q] * terms[q][c * rows:(c + 1) * rows]
+                        total = total.astype(jnp.bfloat16)
+                        for k in range(some):
+                            at = (p * some + k) * rows
+                            mixed[c, g, at:at + rows, n * B:(n + 1) * B] = total[:, k * B:(k + 1) * B]
+
+    def fetch_first(q, g, n):
+        r = order_ref[g * NPB + n]
+        owner = q * (NB // groups) + r // groups
+        at = lax.rem(r, groups)
+        t, j = owner // half, lax.rem(owner, half)
+        return jnp.concatenate([
+            jnp.concatenate([
+                psi[j, e, k, t, pl.ds(at * tiles, tiles)].reshape(share, B) for e in range(ops)
+            ], 0) for k in range(some)
+        ], 1)
+
+    left_dots(fetch_first)
+    for t in range(bits):
+        pl.semaphore_signal(free_sem, inc=1, device_id=to(base + place(1 << t), o), device_id_type=MESH)
+    pl.semaphore_signal(free_sem, inc=1, device_id=to(bond, other), device_id_type=MESH)
+
+    for s in range(streams):
+        for c in range(paints):
+            for mask in range(half):
+                right_ensure(s, c, mask)
+    for copy in right_exchange:
+        copy.wait_send()
+    for copy in right_copies.values():
+        copy.wait_send()
+    for target, copy in left_targets:
+        @pl.when(target != bond)
+        def _():
+            copy.wait_send()
+
+    def right_dots(g):
+        total = None
+        for c in range(channels):
+            source = lax.rem(g + shift_ref[c], NQ)
+            term = lax.dot_general(
+                mixed[c, source], right[c, g], (((1,), (1,)), ((), ())),
+                preferred_element_type=jnp.float32,
+            )
+            total = term if total is None else total + term
+        return total
+
+    own_half = DP // ops * some * rows
+
+    @pl.loop(0, NQ)
+    def _(g):
+        for c in range(channels):
+            for u in range(bonds // 2):
+                pair = [gathered[2 * u + t, c, g].astype(jnp.float32) for t in range(2)]
+                for m in range(NPB):
+                    at = m * B + u * sub
+                    right[c, g, at:at + sub] = jnp.concatenate(
+                        [x[m * fine:(m + 1) * fine] for x in pair], 0).astype(jnp.bfloat16)
+        total = right_dots(g)
+        for e in range(ops):
+            part_sum[g, e] = total[e * own_half:(e + 1) * own_half]
+        remote(part_sum.at[g, other], got_first.at[g], osend.at[g], orecv.at[g], bond, other).start()
+
+    pl.semaphore_wait(free_sem, bits + 1)
+
+    @pl.loop(0, NQ)
+    def _(g):
+        remote(part_sum.at[g, other], got_first.at[g], osend.at[g], orecv.at[g], bond, other).wait()
+        total = (part_sum[g, o] + got_first[g]).astype(jnp.bfloat16)
+        for p in range(DP // ops):
+            for k in range(some):
+                for m in range(NPB):
+                    at = ((p * some + k) * NPB + m) * sub
+                    for n in range(NPB):
+                        psi[i, o, k, p, m * NB + g * NPB + n] = total[at:at + sub, n * B:(n + 1) * B]
+
+    again_step, again_finish = spread((0, 1), [])
+    again_step(0, 0)
+    again_step(1, 0)
+    for n in range(1, bits):
+        again_step(0, n)
+        again_step(1, n)
+    again_finish()
+
+    holder = turn(i)
+    wanted = psi.at[holder, o, :, :, pl.ds((1 - part) * NB, NB)]
+    trade = remote(wanted, swap, wsend, wrecv, partner, o)
+    trade.start()
+
+    def slot_of(x):
+        return lax.rem(2 * x, half) + (2 * x) // half if not isinstance(x, int) else (2 * x) % half + (2 * x) // half
+
+    def fetch_second(q, g, n):
+        per = DP // ops
+        return jnp.concatenate([
+            jnp.concatenate([
+                psi[slot_of(x), q // per, k, q % per, m * NB + g * NPB + n]
+                for m in range(NPB) for x in range(half)
+            ], 0) for k in range(some)
+        ], 1)
+
+    left_dots(fetch_second)
+
+    @pl.loop(0, NQ)
+    def _(g):
+        total = right_dots(g)
+        for x in range(DP * some):
+            for m in range(NPB):
+                at = x * rows + m * sub
+                part_sum[g, m, x * sub:(x + 1) * sub] = total[at:at + sub]
+        remote(part_sum.at[g, other], got_second.at[g], osend2.at[g], orecv2.at[g], bond, other).start()
+
+    @pl.loop(0, NQ)
+    def _(g):
+        remote(part_sum.at[g, other], got_second.at[g], osend2.at[g], orecv2.at[g], bond, other).wait()
+        total = (part_sum[g, o] + got_second[g]).astype(jnp.bfloat16)
+        for n in range(NPB):
+            for x in range(DP * some):
+                sorted_out[g * NPB + n, x] = total[x * sub:(x + 1) * sub, n * B:(n + 1) * B]
+
+    for r in range(NB):
+        s = rank_ref[r]
+        for p in range(DP):
+            for k in range(some):
+                ready[p * (NB // groups) + r // groups, k, r % groups] = sorted_out[s, p * some + k]
+
+    sends = []
+    for e in range(1, bonds):
+        target = lax.rem(bond + e, bonds)
+        copy = remote(ready.at[target], landed.at[bond], asend.at[e], arecv.at[e], target, o)
+        copy.start()
+        sends.append(copy)
+
+    trade.wait()
+    for p in range(DP // ops):
+        for r in range(NB):
+            s = rank_ref[r]
+            for k in range(some):
+                cols = slice((p * NB + r) * B, (p * NB + r + 1) * B)
+                one_ref[part * some + k, :, cols] = psi[
+                    holder, o, k, p, part * NB + s].astype(jnp.float32)
+                one_ref[(1 - part) * some + k, :, cols] = swap[k, p, s].astype(jnp.float32)
+
+    landed[bond] = ready[bond]
+    for copy in sends:
+        copy.wait()
+    for s in range(bonds):
+        x = s % half
+        spot = x // 2 + (x % 2) * (half // 2)
+        for k in range(some):
+            for at in range(groups):
+                two_ref[(s // half) * some + k, spot * sub:(spot + 1) * sub, at * B:(at + 1) * B] = (
+                    landed[s, k, at].astype(jnp.float32))
+
+
+def whole(wave, left_tiles, right_tiles, tables, bonds, ops):
+    roots, sector_rows, strip = wave.shape
+    channels = left_tiles.shape[0]
+    half = bonds // 2
+    bits = half.bit_length() - 1
+    some = roots // 2
+    fine = left_tiles.shape[3]
+    sub = 2 * fine
+    rows = NPB * sub
+    share = sector_rows // ops
+    groups = strip // B
+    height = DP * some * rows
+    paints = 4
+    vmem = pl.BlockSpec(memory_space=pltpu.VMEM)
+    smem = pl.BlockSpec(memory_space=pltpu.SMEM)
+    dma = pltpu.SemaphoreType.DMA
+    bf, f32 = jnp.bfloat16, jnp.float32
+    return pl.pallas_call(
+        functools.partial(whole_kernel, half, ops, some, channels, site_charge_table),
+        out_shape=[
+            jax.ShapeDtypeStruct((roots, NPB * B // bonds, DP // ops * NB * B), f32),
+            jax.ShapeDtypeStruct((roots, share, strip), f32),
+        ],
+        in_specs=[smem] * 6 + [pl.BlockSpec(memory_space=pl.ANY), vmem, vmem],
+        out_specs=[vmem, vmem],
+        scratch_shapes=[
+            pltpu.VMEM((half, ops, some, 2, groups * share // sub, sub, B), bf),
+            pltpu.VMEM((bonds, channels, NQ, NPB * fine, NPB * B), bf),
+            pltpu.VMEM((channels, NQ, NPB * B, NPB * B), bf),
+            pltpu.VMEM((NQ, channels * rows, NPB * B), bf),
+            pltpu.VMEM((2,) + left_tiles.shape, bf),
+            pltpu.VMEM((channels, NQ, height, NPB * B), bf),
+            pltpu.VMEM((NQ, ops, height // ops, NPB * B), f32),
+            pltpu.VMEM((NQ, height // ops, NPB * B), f32),
+            pltpu.VMEM((NQ, height // ops, NPB * B), f32),
+            pltpu.VMEM((roots, share, strip), f32),
+            pltpu.VMEM((some, groups * share // sub, sub, B), bf),
+            pltpu.VMEM((some, DP // ops, NB, sub, B), bf),
+            pltpu.VMEM((NB, DP * some, sub, B), bf),
+            pltpu.VMEM((bonds, some, groups, sub, B), bf),
+            pltpu.VMEM((bonds, some, groups, sub, B), bf),
+            dma, dma((some,)), dma((some,)),
+            dma((2, some, half)), dma((2, some, half)), dma((2, some, half)), dma((2, some, half)),
+            dma((paints,)), dma((paints,)), dma((2, paints, half)), dma((2, paints, half)),
+            dma((2,)), dma((2,)), dma,
+            dma((NQ,)), dma((NQ,)), dma((NQ,)), dma((NQ,)),
+            dma, dma, dma((bonds,)), dma((bonds,)),
+            pltpu.SemaphoreType.REGULAR,
+        ],
+        compiler_params=pltpu.CompilerParams(
+            collective_id=3, has_side_effects=True, vmem_limit_bytes=67043328
+        ),
+        name="whole",
+    )(*tables, wave, left_tiles, right_tiles)
+
+
+def ordering(charge):
+    at = jnp.arange(charge.shape[-1], dtype=jnp.int32)
+    mine, theirs = charge[..., :, None], charge[..., None, :]
+    before = (theirs < mine) | ((theirs == mine) & (at[None, :] < at[:, None]))
+    rank = jnp.sum(before.astype(jnp.int32), -1)
+    order = jnp.sum(jnp.where(rank[..., None, :] == at[:, None], at[None, :], 0), -1)
+    return order, rank
+
+
+def local_whole(
+    wavefunction, left_tiles, right_tiles, site_operators, left_charge, right_charge, channel_charge
+):
+    channels = site_operators.shape[0]
+    op = lax.axis_index("op")
+    own_charge = lax.dynamic_slice_in_dim(channel_charge, op * channels, channels, 0)
+    left_order, unused = ordering(left_charge)
+    right_order, right_rank = ordering(right_charge)
+    shift = (own_charge[:, 0] + own_charge[:, 1] + NQ) % NQ
+    site = site_masks(site_operators, own_charge).reshape(-1)
+    tables = (right_order, right_rank, left_order, shift, own_charge[:, 0] % NQ, site)
+    return tuple(whole(
+        wavefunction, left_tiles, right_tiles, tables, lax.axis_size("bond"), lax.axis_size("op")
+    ))
+
+
+def fits(mesh, wavefunction, left_tiles):
+    bonds, ops = mesh.shape["bond"], mesh.shape["op"]
+    strip = wavefunction.shape[2] // bonds
+    fine = left_tiles.shape[3] // bonds
+    channels = left_tiles.shape[0] // ops
+    return (
+        ops == NPB and bonds == NB and strip % B == 0 and 2 * fine * (bonds // 2) == B
+        and channels % 4 == 0 and NPB * fine == 16
+    )
+
+
 def local(
     wavefunction, left_tiles, right_tiles, site_operators, left_charge, right_charge, channel_charge
 ):
@@ -352,18 +843,22 @@
 
 
 def solution(mesh):
-    return jax.shard_map(
-        local,
-        mesh=mesh,
-        in_specs=(
-            P(None, None, "bond"),
-            P("op", None, None, "bond", None),
-            P("op", None, None, "bond", None),
-            P("op", None, None),
-            P(),
-            P(),
-            P(),
-        ),
-        out_specs=(P(None, "bond", "op"), P(None, "op", "bond")),
-        check_vma=False,
-    )
+    def run(*args):
+        body = local_whole if fits(mesh, args[0], args[1]) else local
+        return jax.shard_map(
+            body,
+            mesh=mesh,
+            in_specs=(
+                P(None, None, "bond"),
+                P("op", None, None, "bond", None),
+                P("op", None, None, "bond", None),
+                P("op", None, None),
+                P(),
+                P(),
+                P(),
+            ),
+            out_specs=(P(None, "bond", "op"), P(None, "op", "bond")),
+            check_vma=False,
+        )(*args)
+
+    return run

time: 354 us -> 257 us (0.73)
  waiting for transfers between devices: 90.1 us -> 0 us
  Pallas kernels: 193 us -> 246 us
  local copies, waits for them, and re-layouts: 30.8 us -> 5.42 us
  between operations: 14.3 us -> 0.66 us
  starting transfers between devices: 12.2 us -> 0 us
  other arithmetic: 10.9 us -> 4.58 us
    all_gather x1 -> x0, waiting for transfers between devices: 66.3 us -> none  [local(): lax.all_gather(right, 'bond', axis=2, tiled=True)]
    pallas_call x4 -> x1, Pallas kernels: 193 us -> 246 us  [whole(): pl.pallas_call(functools.partial(whole_kernel, half, ops, some, channels,...]
    all_to_all x1 -> x0, waiting for transfers between devices: 17.2 us -> none  [local(): lax.all_to_all(second, 'bond', split_axis=0, concat_axis=0, tiled=True)]
    all_to_all x1 -> x0, starting transfers between devices: 6.77 us -> none  [local(): lax.all_to_all(second, 'bond', split_axis=0, concat_axis=0, tiled=True)]
    ppermute x4 -> x0, waiting for transfers between devices: 6.67 us -> none  [the longest x2 6.66 us: summed_share(): total += lax.ppermute(sent, 'op', [(o, (o + e) % ops) for o in range(ops)])]
    reshape x5 -> x1, local copies, waits for them, and re-layouts: 7.01 us -> 0.63 us  [local_whole(): site = site_masks(site_operators, own_charge).reshape(-1)]
    gather x5 -> x0, local copies, waits for them, and re-layouts: 5.92 us -> none  [the longest x4 3.45 us: local(): left = left[jnp.arange(channels)[None, :, None], left_order[left_slots]]]
    ppermute x4 -> x0, starting transfers between devices: 5.38 us -> none  [the longest x1 3.49 us: local(): one = lax.ppermute(left_tiles, 'bond', even)]
  transfers between devices with their start and end apart: 6 -> 0, of which waited for: 4 -> 0; matrix products, arithmetic and copies ran while one was open for 5% -> 0% of each run, Pallas kernels for 25% -> 0%
where the time goes in v1:
time: 257 us
  Pallas kernels  246 us (96%)
  local copies, waits for them, and re-layouts  5.42 us (2%)
  other arithmetic  4.58 us (2%)
    pallas_call x1, Pallas kernels, whole(): pl.pallas_call(functools.partial(whole_kernel, half, ops, some, channels,...  246 us

profile of v1, /device:TPU:14, one launch (start us, length us, event | category | flops | bytes accessed | tf_op | source)
XLA Modules:
  0.0 256.8 jit_solution(3139104903239316873)
XLA Ops:
  0.6 0.9 convert_reduce_fusion.1.rank_ref
  1.5 0.0 copy-start.1
  1.6 0.8 constant_dynamic-slice_fusion
  2.3 0.6 and_select_fusion
  2.9 0.9 convert_reduce_fusion
  3.8 0.6 select_reduce_fusion
  4.5 0.7 broadcast_add_fusion
  5.2 0.0 copy-done.1
  5.2 0.8 fusion.6
  6.0 0.1 copy.12
  6.1 0.6 reshape.41.site_ref
  6.7 246.2 %whole.1 = (f32[6,16,4096]{2,1,0:T(8,128)}, f32[6,128,512]{2,1,0:T(8,128)}) custom-call(s32[16]{0:T(128)} %get-tuple-element.5.order_ref, s32[16]{0:T(128)} %copy-done.1, s32[16]{0:T(128)} %get-tuple-element.4.left_order_ref, s32[8]{0:T(128)} %get-tuple-element.3.shift_ref, s32[8]{0:T(128)} %get-tuple-element.2.left_shift_ref, f32[128]{0:T(128)} %reshape.41.site_ref, ...), custom_call_target="tpu_custom_call" | custom-call | tf_op jit(solution)/shard_map/whole/pallas_call | solution.py:639
  252.9 0.0 copy-start
  252.9 2.8 %copy.15 = f32[6,16,4096]{2,1,0:T(8,128)} copy(f32[6,16,4096]{2,1,0:T(8,128)} %get-tuple-element.8) | data formatting | bytes 3145728
  255.7 0.0 copy-done
  255.7 1.1 copy.16
  (1 shorter events, 0.0 us)
Async XLA Ops:
  1.5 3.7 %copy-start.1 = (s32[16]{0:T(128)}, s32[16]{0:T(128)S(1)}, u32[]{:S(2)}) copy-start(s32[16]{0:T(128)S(1)} %convert_reduce_fusion.1.rank_ref) | copy-start | bytes 196
  252.9 2.8 %copy-start = (f32[6,128,512]{2,1,0:T(8,128)S(1)}, f32[6,128,512]{2,1,0:T(8,128)}, u32[]{:S(2)}) copy-start(f32[6,128,512]{2,1,0:T(8,128)} %get-tuple-element.9) | copy-start | bytes 4718596

commit v2 on v1

--- a/solution.py
+++ b/solution.py
@@ -220,10 +220,66 @@
     )(order, shift, site, psi, left, right)
 
 
+def timetable(bits, psi_orders, right_orders, psi_parts, left_parts, slot, delay, prepared):
+    orders = {"psi": psi_orders, "right": right_orders}
+    waiting, done = [], []
+    landed = 0.0
+
+    def open_node(family, s, c, mask, level, at):
+        for n in range(level, bits):
+            waiting.append((family, s, c, mask, n, at))
+
+    for c in range(len(psi_orders[0])):
+        open_node("psi", 0, c, 0, 0, 0.0)
+    for c in range(len(right_orders[0])):
+        open_node("right", 0, c, 0, 0, prepared)
+    far = [("psi", c) for c in range(psi_parts)] + [("left", c) for c in range(left_parts)]
+    far += [("right", c) for c in range(len(right_orders[0]))]
+    free = [0.0] * bits
+    far_free, now = 0.0, 0.0
+    while waiting or far:
+        for link in range(bits):
+            if free[link] > now:
+                continue
+            if link == bits - 1 and far and far_free <= now:
+                kind, c = far.pop(0)
+                if kind != "right" or now >= prepared:
+                    done.append((now, ("far", kind, c, 0)))
+                    done.append((now + slot, ("far", kind, c, 1)))
+                    free[link] = now + slot
+                    far_free = now + 2 * slot
+                    if kind != "left":
+                        open_node(kind, 1, c, 0, 0, now + 2 * slot + 2 * delay)
+                    continue
+                far.insert(0, (kind, c))
+            best = None
+            for item in waiting:
+                family, s, c, mask, n, at = item
+                if orders[family][s][c][n] != link or at > now:
+                    continue
+                key = (family == "right", n - bits if n < bits - 1 else 0, n, at, s, c, mask)
+                if best is None or key < best[0]:
+                    best = (key, item)
+            if best is None:
+                continue
+            family, s, c, mask, n, at = best[1]
+            waiting.remove(best[1])
+            done.append((now, ("hop", family, s, c, mask, n)))
+            free[link] = now + slot
+            arrival = now + slot + delay
+            if family == "psi":
+                landed = max(landed, arrival)
+            open_node(family, s, c, mask | 1 << link, n + 1, arrival)
+        now += slot / 16
+    done.sort(key=lambda entry: entry[0])
+    return done, landed, now + slot
+
+
 def whole_kernel(
     half, ops, some, channels, site_charges,
-    order_ref, rank_ref, left_order_ref, shift_ref, left_shift_ref, site_ref,
+    left_charge_ref, right_charge_ref, channel_ref, operator_ref,
     wave_ref, lt_ref, rt_ref, one_ref, two_ref,
+    order_ref, rank_ref, left_order_ref, left_rank_ref, shift_ref, left_shift_ref, site_ref,
     psi, gathered, right, left, left_raw, mixed, part_sum, got_first, got_second, stage, away,
     swap, sorted_out, ready, landed,
     stage_sem, psend, precv, send_sem, recv_sem, fsend, frecv,
@@ -287,7 +343,7 @@
                 ].astype(jnp.bfloat16)
     pl.semaphore_wait(barrier, bonds)
 
-    def spread(index, exchange):
+    def spread(index, exchange, orders):
         colours = some
         copies, forwards, ready_set = {}, [], set()
 
@@ -307,21 +363,18 @@
             copy.start()
             forwards.append(copy)
 
-        reached = [[[0] for c in range(colours)] for s in range(streams)]
+        def hop(s, c, mask, n):
+            bit = 1 << orders[s][c][n]
+            ensure(s, c, mask)
+            copy = remote(slot(s, c, mask), slot(s, c, mask), send_sem.at[s, c, mask | bit],
+                          recv_sem.at[s, c, mask | bit], base + place(bit), o)
+            copy.start()
+            copies[s, c, mask | bit] = copy
 
         def step(s, n):
             for at in range(1 << n):
                 for c in range(colours):
-                    mask = reached[s][c][at]
-                    bit = 1 << (c + n) % bits
-                    ensure(s, c, mask)
-                    copy = remote(slot(s, c, mask), slot(s, c, mask), send_sem.at[s, c, mask | bit],
-                                  recv_sem.at[s, c, mask | bit], base + place(bit), o)
-                    copy.start()
-                    copies[s, c, mask | bit] = copy
-            for c in range(colours):
-                bit = 1 << (c + n) % bits
-                reached[s][c] = reached[s][c] + [mask | bit for mask in reached[s][c]]
+                    hop(s, c, sum(1 << orders[s][c][b] for b in range(n) if at >> b & 1), n)
 
         def finish():
             for s in range(streams):
@@ -335,14 +388,117 @@
             for copy in forwards:
                 copy.wait()
 
-        return step, finish
+        return hop, step, finish
 
     exchange = []
     for c in range(some):
         exchange.append(remote(away.at[c], psi.at[i, o, c, part], psend.at[c], precv.at[c], partner, o))
-        exchange[-1].start()
-    psi_step, psi_finish = spread((part, 1 - part), exchange)
-    psi_step(0, 0)
+    last = bits - 1
+    turns = [(0, 1, last), (1, last, 0), (last, 0, 1)]
+    psi_orders = [turns, [(0, last, 1), (1, last, 0), (last, 1, 0)]]
+    right_orders = [[(last, 0, 1), (last, 1, 0), (0, last, 1), (1, last, 0)]] * 2
+    paints = len(right_orders[0])
+    wide = channels // paints
+    psi_hop, unused, psi_finish = spread((part, 1 - part), exchange, psi_orders)
+    plan, psi_landed, plan_end = timetable(
+        bits, psi_orders, right_orders, some, paints, 2.8, 2.5, 6.0)
+    plan = list(plan)
+
+    def lead(until):
+        while plan and plan[0][0] <= until:
+            operation = plan.pop(0)[1]
+            if operation[0] == "far":
+                send_far(*operation[1:])
+            elif operation[1] == "psi":
+                psi_hop(*operation[2:])
+            else:
+                right_hop(*operation[2:])
+
+    def send_far(kind, c, turn_of):
+        if kind == "psi":
+            item = [(None, exchange[c])]
+        elif kind == "right":
+            item = [(None, right_exchange[c])]
+        else:
+            item = left_copies[2 * c:2 * c + 2] + own_left[c:c + 1]
+        ready_now = lax.rem(part + i // (half // 2), 2) == turn_of
+        for when, copy in item:
+            @pl.when(ready_now if when is None else when & ready_now)
+            def _():
+                copy.start()
+
+    def tile(slot, c):
+        return gathered.at[slot, pl.ds(c * wide, wide)]
+
+    right_exchange = []
+    for c in range(paints):
+        right_exchange.append(remote(tile(bond, c), tile(bond, c), rpsend.at[c], rprecv.at[c], partner, o))
+    right_copies, right_ready = {}, set()
+
+    def right_ensure(s, c, mask):
+        if (s, c, mask) in right_ready:
+            return
+        right_ready.add((s, c, mask))
+        if mask:
+            right_copies[s, c, mask].wait_recv()
+        elif s == 1:
+            right_exchange[c].wait_recv()
+
+    def right_hop(s, c, mask, n):
+        start = base if s == 0 else half - base
+        bit = 1 << right_orders[s][c][n]
+        right_ensure(s, c, mask)
+        here = tile(start + place(mask), c)
+        copy = remote(here, here, rsend.at[s, c, mask | bit], rrecv.at[s, c, mask | bit],
+                      base + place(bit), o)
+        copy.start()
+        right_copies[s, c, mask | bit] = copy
+
+    parity = lax.rem(bond, 2)
+
+    def left_part(ref, c):
+        return ref.at[pl.ds(c * wide, wide)]
+
+    left_copies, own_left = [], []
+    for c in range(paints):
+        for h in range(2):
+            target = h * half + turn(bond // 2)
+            left_copies.append((target != bond, remote(
+                left_part(lt_ref, c), left_part(left_raw.at[parity], c),
+                lsend.at[h, c], lrecv.at[parity, c], target, o)))
+        own_left.append((lax.rem(turn(bond // 2), half) == i, pltpu.make_async_copy(
+            left_part(lt_ref, c), left_part(left_raw.at[parity], c), lown.at[c])))
+
+    lead(2.0)
+    for ref, order, rank in ((right_charge_ref, order_ref, rank_ref),
+                             (left_charge_ref, left_order_ref, left_rank_ref)):
+        @pl.loop(0, NB)
+        def _(b):
+            mine = ref[b]
+            total = jnp.int32(0)
+            for e in range(NB):
+                ahead = (ref[e] < mine) | ((ref[e] == mine) & (e < b))
+                total += jnp.where(ahead, 1, 0)
+            rank[b] = total
+
+        @pl.loop(0, NB)
+        def _(b):
+            total = jnp.int32(0)
+            for e in range(NB):
+                total += jnp.where(rank[e] == b, e, 0)
+            order[b] = total
+
+    @pl.loop(0, channels)
+    def _(c):
+        left_shift = channel_ref[o * channels + c, 0]
+        move = channel_ref[o * channels + c, 1]
+        left_shift_ref[c] = lax.rem(left_shift + NQ, NQ)
+        shift_ref[c] = lax.rem(left_shift + move + 2 * NQ, NQ)
+        for p in range(DP):
+            for q in range(DP):
+                gap = site_charges[p] - site_charges[q] - move + 4 * NQ
+                site_ref[(c * DP + p) * DP + q] = jnp.where(
+                    lax.rem(gap, NQ) == 0, operator_ref[c, p, q], 0.0)
 
     @pl.loop(0, channels)
     def _(c):
@@ -354,86 +510,19 @@
                     [rt_ref[c, r, n].astype(jnp.float32) for n in range(NPB)], 1))
             gathered[bond, c, g] = jnp.concatenate(bands, 0).astype(jnp.bfloat16)
 
-    last = bits - 1
-    orders = [(last, 0, 1), (last, 1, 0), (0, last, 1), (1, last, 0)]
-    paints = len(orders)
-    wide = channels // paints
-
-    def tile(slot, c):
-        return gathered.at[slot, pl.ds(c * wide, wide)]
-
-    right_exchange = []
-    for c in range(paints):
-        right_exchange.append(remote(tile(bond, c), tile(bond, c), rpsend.at[c], rprecv.at[c], partner, o))
-    right_copies, right_ready = {}, set()
-
-    def right_ensure(s, c, mask):
-        if (s, c, mask) in right_ready:
-            return
-        right_ready.add((s, c, mask))
-        if mask:
-            right_copies[s, c, mask].wait_recv()
-        elif s == 1:
-            right_exchange[c].wait_recv()
-
-    right_reached = [[[0] for c in range(paints)] for s in range(streams)]
-
-    def right_step(s, n):
-        start = base if s == 0 else half - base
-        for at in range(1 << n):
-            for c in range(paints):
-                mask = right_reached[s][c][at]
-                bit = 1 << orders[c][n]
-                right_ensure(s, c, mask)
-                here = tile(start + place(mask), c)
-                copy = remote(here, here, rsend.at[s, c, mask | bit], rrecv.at[s, c, mask | bit],
-                              base + place(bit), o)
-                copy.start()
-                right_copies[s, c, mask | bit] = copy
-        for c in range(paints):
-            bit = 1 << orders[c][n]
-            right_reached[s][c] = right_reached[s][c] + [mask | bit for mask in right_reached[s][c]]
-
-    for copy in right_exchange:
-        copy.start()
-    parity = lax.rem(bond, 2)
-    left_targets = []
-    for h in range(2):
-        target = h * half + turn(bond // 2)
-        left_targets.append((target, remote(
-            lt_ref, left_raw.at[parity], lsend.at[h], lrecv.at[parity], target, o)))
-    own_left = pltpu.make_async_copy(lt_ref, left_raw.at[parity], lown)
-    for target, copy in left_targets:
-        @pl.when(target != bond)
-        def _():
-            copy.start()
-
-        @pl.when(target == bond)
-        def _():
-            own_left.start()
-
-    right_step(0, 0)
-    psi_step(0, 1)
-    psi_step(0, 2)
-    right_step(0, 1)
-    psi_step(1, 0)
-    psi_step(1, 1)
-    psi_step(1, 2)
-    right_step(0, 2)
-    right_step(1, 0)
-    right_step(1, 1)
-
+    lead(psi_landed)
     band = i // 2 + lax.rem(i, 2) * (half // 2)
     for t in range(2):
         source = 2 * band + t
-
-        @pl.when(source != bond)
-        def _():
-            remote(lt_ref, left_raw.at[t], lsend.at[0], lrecv.at[t], source, o).wait_recv()
-
-        @pl.when(source == bond)
-        def _():
-            own_left.wait()
+        for c in range(paints):
+            @pl.when(source != bond)
+            def _():
+                remote(left_part(lt_ref, c), left_part(left_raw.at[t], c), lsend.at[0, c],
+                       lrecv.at[t, c], source, o).wait_recv()
+
+            @pl.when(source == bond)
+            def _():
+                own_left[c][1].wait()
 
     @pl.loop(0, NQ)
     def _(h):
@@ -448,11 +537,10 @@
                 at = c * rows + m * sub
                 left[h, at:at + sub] = jnp.concatenate(pieces, 0).astype(jnp.bfloat16)
 
-    right_step(1, 2)
     psi_finish()
 
-    def left_dots(fetch):
-        @pl.loop(0, NQ)
+    def left_dots(fetch, first, count):
+        @pl.loop(first, first + count)
         def _(g):
             for n in range(NPB):
                 terms = []
@@ -482,7 +570,11 @@
             ], 0) for k in range(some)
         ], 1)
 
-    left_dots(fetch_first)
+    slices = NQ // 2
+    for g in range(slices):
+        left_dots(fetch_first, g * NQ // slices, NQ // slices)
+        lead(psi_landed + (g + 1) * (plan_end - psi_landed) / slices)
+    lead(plan_end)
     for t in range(bits):
         pl.semaphore_signal(free_sem, inc=1, device_id=to(base + place(1 << t), o), device_id_type=MESH)
     pl.semaphore_signal(free_sem, inc=1, device_id=to(bond, other), device_id_type=MESH)
@@ -495,8 +587,8 @@
         copy.wait_send()
     for copy in right_copies.values():
         copy.wait_send()
-    for target, copy in left_targets:
-        @pl.when(target != bond)
+    for away_from_here, copy in left_copies:
+        @pl.when(away_from_here)
         def _():
             copy.wait_send()
 
@@ -540,7 +632,7 @@
                     for n in range(NPB):
                         psi[i, o, k, p, m * NB + g * NPB + n] = total[at:at + sub, n * B:(n + 1) * B]
 
-    again_step, again_finish = spread((0, 1), [])
+    unused, again_step, again_finish = spread((0, 1), [], [turns, turns])
     again_step(0, 0)
     again_step(1, 0)
     for n in range(1, bits):
@@ -565,7 +657,7 @@
             ], 0) for k in range(some)
         ], 1)
 
-    left_dots(fetch_second)
+    left_dots(fetch_second, 0, NQ)
 
     @pl.loop(0, NQ)
     def _(g):
@@ -642,9 +734,10 @@
             jax.ShapeDtypeStruct((roots, NPB * B // bonds, DP // ops * NB * B), f32),
             jax.ShapeDtypeStruct((roots, share, strip), f32),
         ],
-        in_specs=[smem] * 6 + [pl.BlockSpec(memory_space=pl.ANY), vmem, vmem],
+        in_specs=[smem] * 4 + [pl.BlockSpec(memory_space=pl.ANY), vmem, vmem],
         out_specs=[vmem, vmem],
-        scratch_shapes=[
+        scratch_shapes=[pltpu.SMEM((NB,), jnp.int32)] * 4 + [pltpu.SMEM((channels,), jnp.int32)] * 2 + [
+            pltpu.SMEM((channels * DP * DP,), f32),
             pltpu.VMEM((half, ops, some, 2, groups * share // sub, sub, B), bf),
             pltpu.VMEM((bonds, channels, NQ, NPB * fine, NPB * B), bf),
             pltpu.VMEM((channels, NQ, NPB * B, NPB * B), bf),
@@ -663,7 +756,7 @@
             dma, dma((some,)), dma((some,)),
             dma((2, some, half)), dma((2, some, half)), dma((2, some, half)), dma((2, some, half)),
             dma((paints,)), dma((paints,)), dma((2, paints, half)), dma((2, paints, half)),
-            dma((2,)), dma((2,)), dma,
+            dma((2, paints)), dma((2, paints)), dma((paints,)),
             dma((NQ,)), dma((NQ,)), dma((NQ,)), dma((NQ,)),
             dma, dma, dma((bonds,)), dma((bonds,)),
             pltpu.SemaphoreType.REGULAR,
@@ -675,26 +768,10 @@
     )(*tables, wave, left_tiles, right_tiles)
 
 
-def ordering(charge):
-    at = jnp.arange(charge.shape[-1], dtype=jnp.int32)
-    mine, theirs = charge[..., :, None], charge[..., None, :]
-    before = (theirs < mine) | ((theirs == mine) & (at[None, :] < at[:, None]))
-    rank = jnp.sum(before.astype(jnp.int32), -1)
-    order = jnp.sum(jnp.where(rank[..., None, :] == at[:, None], at[None, :], 0), -1)
-    return order, rank
-
-
 def local_whole(
     wavefunction, left_tiles, right_tiles, site_operators, left_charge, right_charge, channel_charge
 ):
-    channels = site_operators.shape[0]
-    op = lax.axis_index("op")
-    own_charge = lax.dynamic_slice_in_dim(channel_charge, op * channels, channels, 0)
-    left_order, unused = ordering(left_charge)
-    right_order, right_rank = ordering(right_charge)
-    shift = (own_charge[:, 0] + own_charge[:, 1] + NQ) % NQ
-    site = site_masks(site_operators, own_charge).reshape(-1)
-    tables = (right_order, right_rank, left_order, shift, own_charge[:, 0] % NQ, site)
+    tables = (left_charge, right_charge, channel_charge, site_operators)
     return tuple(whole(
         wavefunction, left_tiles, right_tiles, tables, lax.axis_size("bond"), lax.axis_size("op")
     ))

time: 257 us -> 225 us (0.88)
  Pallas kernels: 246 us -> 218 us
  other arithmetic: 4.58 us -> 0 us
    pallas_call x1, Pallas kernels: 246 us -> 218 us  [whole(): pl.pallas_call(functools.partial(whole_kernel, half, ops, some, channels,...]
    unnamed x6, local copies, waits for them, and re-layouts: 3.92 us -> 6.66 us
where the time goes in v2:
time: 225 us
  Pallas kernels  218 us (97%)
  local copies, waits for them, and re-layouts  6.66 us (3%)
    pallas_call x1, Pallas kernels, whole(): pl.pallas_call(functools.partial(whole_kernel, half, ops, some, channels,...  218 us
    unnamed x6, local copies, waits for them, and re-layouts  6.66 us

profile of v2, /device:TPU:14, one launch (start us, length us, event | category | flops | bytes accessed | tf_op | source)
XLA Modules:
  0.0 225.2 jit_solution(1015246202792057153)
XLA Ops:
  0.6 1.4 copy.9.channel_ref
  2.0 1.4 copy.10.operator_ref
  3.4 217.9 %whole.1 = (f32[6,16,4096]{2,1,0:T(8,128)}, f32[6,128,512]{2,1,0:T(8,128)}) custom-call(s32[16]{0:T(128)} %left_charge_ref.1, s32[16]{0:T(128)} %right_charge_ref.1, s32[16,2]{1,0:T(8,128)} %copy.9.channel_ref, f32[8,4,4]{2,1,0:T(4,128)} %copy.10.operator_ref, f32[6,256,512]{2,1,0:T(8,128)} %wave_ref.1, bf16[8,16,2,8,128]{4,3,2,1,0:T(8,128)(2,1)} %lt_ref.1, ...), custom_call_target="tpu_custom_call" | custom-call | tf_op jit(solution)/shard_map/whole/pallas_call | solution.py:731
  221.3 0.0 copy-start
  221.3 2.8 %copy.13 = f32[6,16,4096]{2,1,0:T(8,128)} copy(f32[6,16,4096]{2,1,0:T(8,128)} %get-tuple-element.4) | data formatting | bytes 3145728
  224.1 0.0 copy-done
  224.1 1.1 copy.14
Async XLA Ops:
  221.3 2.8 %copy-start = (f32[6,128,512]{2,1,0:T(8,128)S(1)}, f32[6,128,512]{2,1,0:T(8,128)}, u32[]{:S(2)}) copy-start(f32[6,128,512]{2,1,0:T(8,128)} %get-tuple-element.5) | copy-start | bytes 4718596

commit v3 on v2

--- a/solution.py
+++ b/solution.py
@@ -279,7 +279,7 @@
     half, ops, some, channels, site_charges,
     left_charge_ref, right_charge_ref, channel_ref, operator_ref,
     wave_ref, lt_ref, rt_ref, one_ref, two_ref,
-    order_ref, rank_ref, left_order_ref, left_rank_ref, shift_ref, left_shift_ref, site_ref,
+    order_ref, rank_ref, left_order_ref, left_rank_ref, shift_ref, left_shift_ref, site_ref, pick_ref, products,
     psi, gathered, right, left, left_raw, mixed, part_sum, got_first, got_second, stage, away,
     swap, sorted_out, ready, landed,
     stage_sem, psend, precv, send_sem, recv_sem, fsend, frecv,
@@ -298,6 +298,7 @@
     sub = rows // NPB
     fine = lt_ref.shape[3]
     streams = 2
+    most = max(site_charges.count(x) for x in site_charges)
     other = lax.rem(o + 1, ops)
 
     def place(mask):
@@ -343,12 +344,12 @@
                 ].astype(jnp.bfloat16)
     pl.semaphore_wait(barrier, bonds)
 
-    def spread(index, exchange, orders):
+    def spread(view, exchange, orders):
         colours = some
-        copies, forwards, ready_set = {}, [], set()
+        copies, forwards, ready_set = {}, [[], []], set()
 
         def slot(s, c, mask):
-            return psi.at[place(mask), o, c, index[s]]
+            return view(place(mask), c, s)
 
         def ensure(s, c, mask):
             if (s, c, mask) in ready_set:
@@ -361,7 +362,7 @@
             copy = remote(slot(s, c, mask), slot(s, c, mask), fsend.at[s, c, mask],
                           frecv.at[s, c, mask], bond, other)
             copy.start()
-            forwards.append(copy)
+            forwards[s].append(copy)
 
         def hop(s, c, mask, n):
             bit = 1 << orders[s][c][n]
@@ -376,19 +377,22 @@
                 for c in range(colours):
                     hop(s, c, sum(1 << orders[s][c][b] for b in range(n) if at >> b & 1), n)
 
+        def arrive(s):
+            for mask in range(half):
+                for c in range(colours):
+                    ensure(s, c, mask)
+            while forwards[s]:
+                forwards[s].pop().wait()
+
         def finish():
             for s in range(streams):
-                for mask in range(half):
-                    for c in range(colours):
-                        ensure(s, c, mask)
+                arrive(s)
             for copy in copies.values():
                 copy.wait_send()
             for copy in exchange:
                 copy.wait_send()
-            for copy in forwards:
-                copy.wait()
-
-        return hop, step, finish
+
+        return hop, step, arrive, finish
 
     exchange = []
     for c in range(some):
@@ -399,7 +403,10 @@
     right_orders = [[(last, 0, 1), (last, 1, 0), (0, last, 1), (1, last, 0)]] * 2
     paints = len(right_orders[0])
     wide = channels // paints
-    psi_hop, unused, psi_finish = spread((part, 1 - part), exchange, psi_orders)
+    def view_first(j, c, s):
+        return psi.at[j, o, c, part if s == 0 else 1 - part]
+
+    psi_hop, unused, unused, psi_finish = spread(view_first, exchange, psi_orders)
     plan, psi_landed, plan_end = timetable(
         bits, psi_orders, right_orders, some, paints, 2.8, 2.5, 6.0)
     plan = list(plan)
@@ -495,10 +502,20 @@
         left_shift_ref[c] = lax.rem(left_shift + NQ, NQ)
         shift_ref[c] = lax.rem(left_shift + move + 2 * NQ, NQ)
         for p in range(DP):
+            seen = jnp.int32(0)
+            picks = [jnp.int32(0)] * most
+            values = [jnp.float32(0)] * most
             for q in range(DP):
                 gap = site_charges[p] - site_charges[q] - move + 4 * NQ
-                site_ref[(c * DP + p) * DP + q] = jnp.where(
-                    lax.rem(gap, NQ) == 0, operator_ref[c, p, q], 0.0)
+                allowed = lax.rem(gap, NQ) == 0
+                for e in range(most):
+                    here = allowed & (seen == e)
+                    picks[e] = jnp.where(here, q, picks[e])
+                    values[e] = jnp.where(here, operator_ref[c, p, q], values[e])
+                seen += jnp.where(allowed, 1, 0)
+            for e in range(most):
+                site_ref[(c * DP + p) * most + e] = values[e]
+                pick_ref[(c * DP + p) * most + e] = picks[e]
 
     @pl.loop(0, channels)
     def _(c):
@@ -549,11 +566,15 @@
                     terms.append(
                         jnp.dot(left[h], fetch(q, g, n), preferred_element_type=jnp.float32)
                     )
+                for q in range(DP):
+                    products[q] = terms[q]
                 for c in range(channels):
                     for p in range(DP):
-                        total = site_ref[(c * DP + p) * DP] * terms[0][c * rows:(c + 1) * rows]
-                        for q in range(1, DP):
-                            total += site_ref[(c * DP + p) * DP + q] * terms[q][c * rows:(c + 1) * rows]
+                        total = None
+                        for e in range(most):
+                            at = (c * DP + p) * most + e
+                            term = site_ref[at] * products[pick_ref[at], c * rows:(c + 1) * rows]
+                            total = term if total is None else total + term
                         total = total.astype(jnp.bfloat16)
                         for k in range(some):
                             at = (p * some + k) * rows
@@ -619,6 +640,14 @@
             part_sum[g, e] = total[e * own_half:(e + 1) * own_half]
         remote(part_sum.at[g, other], got_first.at[g], osend.at[g], orecv.at[g], bond, other).start()
 
+    span = NB // streams
+
+    def spot_of(s, m):
+        return (s // span * NPB + m) * span + lax.rem(s, span)
+
+    def view_second(j, c, s):
+        return psi.at[j, o, c, :, pl.ds(s * NPB * span, NPB * span)]
+
     pl.semaphore_wait(free_sem, bits + 1)
 
     @pl.loop(0, NQ)
@@ -630,20 +659,13 @@
                 for m in range(NPB):
                     at = ((p * some + k) * NPB + m) * sub
                     for n in range(NPB):
-                        psi[i, o, k, p, m * NB + g * NPB + n] = total[at:at + sub, n * B:(n + 1) * B]
-
-    unused, again_step, again_finish = spread((0, 1), [], [turns, turns])
-    again_step(0, 0)
-    again_step(1, 0)
-    for n in range(1, bits):
+                        psi[i, o, k, p, spot_of(g * NPB + n, m)] = total[at:at + sub, n * B:(n + 1) * B]
+
+    unused, again_step, again_arrive, again_finish = spread(view_second, [], [turns, turns])
+    for n in range(bits):
         again_step(0, n)
         again_step(1, n)
-    again_finish()
-
-    holder = turn(i)
-    wanted = psi.at[holder, o, :, :, pl.ds((1 - part) * NB, NB)]
-    trade = remote(wanted, swap, wsend, wrecv, partner, o)
-    trade.start()
+    again_arrive(0)
 
     def slot_of(x):
         return lax.rem(2 * x, half) + (2 * x) // half if not isinstance(x, int) else (2 * x) % half + (2 * x) // half
@@ -652,12 +674,24 @@
         per = DP // ops
         return jnp.concatenate([
             jnp.concatenate([
-                psi[slot_of(x), q // per, k, q % per, m * NB + g * NPB + n]
+                psi[slot_of(x), q // per, k, q % per, spot_of(g * NPB + n, m)]
                 for m in range(NPB) for x in range(half)
             ], 0) for k in range(some)
         ], 1)
 
-    left_dots(fetch_second, 0, NQ)
+    holder = turn(i)
+    trades = []
+
+    def start_trade(s):
+        wanted = psi.at[holder, o, :, :, pl.ds(s * NPB * span + (1 - part) * span, span)]
+        trades.append(remote(wanted, swap.at[s], wsend.at[s], wrecv.at[s], partner, o))
+        trades[-1].start()
+
+    start_trade(0)
+    left_dots(fetch_second, 0, NQ // streams)
+    again_finish()
+    start_trade(1)
+    left_dots(fetch_second, NQ // streams, NQ // streams)
 
     @pl.loop(0, NQ)
     def _(g):
@@ -689,15 +723,16 @@
         copy.start()
         sends.append(copy)
 
-    trade.wait()
+    for copy in trades:
+        copy.wait()
     for p in range(DP // ops):
         for r in range(NB):
             s = rank_ref[r]
             for k in range(some):
                 cols = slice((p * NB + r) * B, (p * NB + r + 1) * B)
                 one_ref[part * some + k, :, cols] = psi[
-                    holder, o, k, p, part * NB + s].astype(jnp.float32)
-                one_ref[(1 - part) * some + k, :, cols] = swap[k, p, s].astype(jnp.float32)
+                    holder, o, k, p, spot_of(s, part)].astype(jnp.float32)
+                one_ref[(1 - part) * some + k, :, cols] = swap[s // span, k, p, lax.rem(s, span)].astype(jnp.float32)
 
     landed[bond] = ready[bond]
     for copy in sends:
@@ -737,7 +772,8 @@
         in_specs=[smem] * 4 + [pl.BlockSpec(memory_space=pl.ANY), vmem, vmem],
         out_specs=[vmem, vmem],
         scratch_shapes=[pltpu.SMEM((NB,), jnp.int32)] * 4 + [pltpu.SMEM((channels,), jnp.int32)] * 2 + [
-            pltpu.SMEM((channels * DP * DP,), f32),
+            pltpu.SMEM((channels * DP * DP,), f32), pltpu.SMEM((channels * DP * DP,), jnp.int32),
+            pltpu.VMEM((DP, channels * rows, some * B), f32),
             pltpu.VMEM((half, ops, some, 2, groups * share // sub, sub, B), bf),
             pltpu.VMEM((bonds, channels, NQ, NPB * fine, NPB * B), bf),
             pltpu.VMEM((channels, NQ, NPB * B, NPB * B), bf),
@@ -749,7 +785,7 @@
             pltpu.VMEM((NQ, height // ops, NPB * B), f32),
             pltpu.VMEM((roots, share, strip), f32),
             pltpu.VMEM((some, groups * share // sub, sub, B), bf),
-            pltpu.VMEM((some, DP // ops, NB, sub, B), bf),
+            pltpu.VMEM((2, some, DP // ops, NB // 2, sub, B), bf),
             pltpu.VMEM((NB, DP * some, sub, B), bf),
             pltpu.VMEM((bonds, some, groups, sub, B), bf),
             pltpu.VMEM((bonds, some, groups, sub, B), bf),
@@ -758,7 +794,7 @@
             dma((paints,)), dma((paints,)), dma((2, paints, half)), dma((2, paints, half)),
             dma((2, paints)), dma((2, paints)), dma((paints,)),
             dma((NQ,)), dma((NQ,)), dma((NQ,)), dma((NQ,)),
-            dma, dma, dma((bonds,)), dma((bonds,)),
+            dma((2,)), dma((2,)), dma((bonds,)), dma((bonds,)),
             pltpu.SemaphoreType.REGULAR,
         ],
         compiler_params=pltpu.CompilerParams(

time: 225 us -> 225 us (level)
  no operation moved by 1% of the time
where the time goes in v3:
time: 225 us; the launch traced here: 224 us
  Pallas kernels  217 us (96%)
  local copies, waits for them, and re-layouts  6.66 us (3%)
    pallas_call x1, Pallas kernels, whole(): pl.pallas_call(functools.partial(whole_kernel, half, ops, some, channels,...  217 us
    unnamed x6, local copies, waits for them, and re-layouts  6.66 us

profile of v3, /device:TPU:14, one launch (start us, length us, event | category | flops | bytes accessed | tf_op | source)
XLA Modules:
  0.0 224.2 jit_solution(13357676662546442085)
XLA Ops:
  0.6 1.4 copy.9.channel_ref
  2.0 1.4 copy.10.operator_ref
  3.4 216.9 %whole.1 = (f32[6,16,4096]{2,1,0:T(8,128)}, f32[6,128,512]{2,1,0:T(8,128)}) custom-call(s32[16]{0:T(128)} %left_charge_ref.1, s32[16]{0:T(128)} %right_charge_ref.1, s32[16,2]{1,0:T(8,128)} %copy.9.channel_ref, f32[8,4,4]{2,1,0:T(4,128)} %copy.10.operator_ref, f32[6,256,512]{2,1,0:T(8,128)} %wave_ref.1, bf16[8,16,2,8,128]{4,3,2,1,0:T(8,128)(2,1)} %lt_ref.1, ...), custom_call_target="tpu_custom_call" | custom-call | tf_op jit(solution)/shard_map/whole/pallas_call | solution.py:766
  220.3 0.0 copy-start
  220.3 2.8 %copy.13 = f32[6,16,4096]{2,1,0:T(8,128)} copy(f32[6,16,4096]{2,1,0:T(8,128)} %get-tuple-element.4) | data formatting | bytes 3145728
  223.1 0.0 copy-done
  223.1 1.1 copy.14
Async XLA Ops:
  220.3 2.8 %copy-start = (f32[6,128,512]{2,1,0:T(8,128)S(1)}, f32[6,128,512]{2,1,0:T(8,128)}, u32[]{:S(2)}) copy-start(f32[6,128,512]{2,1,0:T(8,128)} %get-tuple-element.5) | copy-start | bytes 4718596

commit v4 on v3

--- a/solution.py
+++ b/solution.py
@@ -279,7 +279,7 @@
     half, ops, some, channels, site_charges,
     left_charge_ref, right_charge_ref, channel_ref, operator_ref,
     wave_ref, lt_ref, rt_ref, one_ref, two_ref,
-    order_ref, rank_ref, left_order_ref, left_rank_ref, shift_ref, left_shift_ref, site_ref, pick_ref, products,
+    order_ref, rank_ref, left_order_ref, left_rank_ref, shift_ref, left_shift_ref, site_ref,
     psi, gathered, right, left, left_raw, mixed, part_sum, got_first, got_second, stage, away,
     swap, sorted_out, ready, landed,
     stage_sem, psend, precv, send_sem, recv_sem, fsend, frecv,
@@ -298,7 +298,6 @@
     sub = rows // NPB
     fine = lt_ref.shape[3]
     streams = 2
-    most = max(site_charges.count(x) for x in site_charges)
     other = lax.rem(o + 1, ops)
 
     def place(mask):
@@ -408,7 +407,7 @@
 
     psi_hop, unused, unused, psi_finish = spread(view_first, exchange, psi_orders)
     plan, psi_landed, plan_end = timetable(
-        bits, psi_orders, right_orders, some, paints, 2.8, 2.5, 6.0)
+        bits, psi_orders, right_orders, some, paints, 2.8, 1.5, 6.0)
     plan = list(plan)
 
     def lead(until):
@@ -502,20 +501,10 @@
         left_shift_ref[c] = lax.rem(left_shift + NQ, NQ)
         shift_ref[c] = lax.rem(left_shift + move + 2 * NQ, NQ)
         for p in range(DP):
-            seen = jnp.int32(0)
-            picks = [jnp.int32(0)] * most
-            values = [jnp.float32(0)] * most
             for q in range(DP):
                 gap = site_charges[p] - site_charges[q] - move + 4 * NQ
-                allowed = lax.rem(gap, NQ) == 0
-                for e in range(most):
-                    here = allowed & (seen == e)
-                    picks[e] = jnp.where(here, q, picks[e])
-                    values[e] = jnp.where(here, operator_ref[c, p, q], values[e])
-                seen += jnp.where(allowed, 1, 0)
-            for e in range(most):
-                site_ref[(c * DP + p) * most + e] = values[e]
-                pick_ref[(c * DP + p) * most + e] = picks[e]
+                site_ref[(c * DP + p) * DP + q] = jnp.where(
+                    lax.rem(gap, NQ) == 0, operator_ref[c, p, q], 0.0)
 
     @pl.loop(0, channels)
     def _(c):
@@ -566,15 +555,11 @@
                     terms.append(
                         jnp.dot(left[h], fetch(q, g, n), preferred_element_type=jnp.float32)
                     )
-                for q in range(DP):
-                    products[q] = terms[q]
                 for c in range(channels):
                     for p in range(DP):
-                        total = None
-                        for e in range(most):
-                            at = (c * DP + p) * most + e
-                            term = site_ref[at] * products[pick_ref[at], c * rows:(c + 1) * rows]
-                            total = term if total is None else total + term
+                        total = site_ref[(c * DP + p) * DP] * terms[0][c * rows:(c + 1) * rows]
+                        for q in range(1, DP):
+                            total += site_ref[(c * DP + p) * DP + q] * terms[q][c * rows:(c + 1) * rows]
                         total = total.astype(jnp.bfloat16)
                         for k in range(some):
                             at = (p * some + k) * rows
@@ -772,8 +757,7 @@
         in_specs=[smem] * 4 + [pl.BlockSpec(memory_space=pl.ANY), vmem, vmem],
         out_specs=[vmem, vmem],
         scratch_shapes=[pltpu.SMEM((NB,), jnp.int32)] * 4 + [pltpu.SMEM((channels,), jnp.int32)] * 2 + [
-            pltpu.SMEM((channels * DP * DP,), f32), pltpu.SMEM((channels * DP * DP,), jnp.int32),
-            pltpu.VMEM((DP, channels * rows, some * B), f32),
+            pltpu.SMEM((channels * DP * DP,), f32),
             pltpu.VMEM((half, ops, some, 2, groups * share // sub, sub, B), bf),
             pltpu.VMEM((bonds, channels, NQ, NPB * fine, NPB * B), bf),
             pltpu.VMEM((channels, NQ, NPB * B, NPB * B), bf),

time: 225 us -> 222 us (0.987)
  Pallas kernels: 217 us -> 214 us
    pallas_call x1, Pallas kernels: 217 us -> 214 us  [whole(): pl.pallas_call(functools.partial(whole_kernel, half, ops, some, channels,...]
where the time goes in v4:
time: 222 us; the launch traced here: 221 us
  Pallas kernels  214 us (96%)
  local copies, waits for them, and re-layouts  6.66 us (3%)
    pallas_call x1, Pallas kernels, whole(): pl.pallas_call(functools.partial(whole_kernel, half, ops, some, channels,...  214 us
    unnamed x6, local copies, waits for them, and re-layouts  6.66 us

profile of v4, /device:TPU:14, one launch (start us, length us, event | category | flops | bytes accessed | tf_op | source)
XLA Modules:
  0.0 221.4 jit_solution(16202658486680736681)
XLA Ops:
  0.6 1.4 copy.9.channel_ref
  2.0 1.4 copy.10.operator_ref
  3.4 214.0 %whole.1 = (f32[6,16,4096]{2,1,0:T(8,128)}, f32[6,128,512]{2,1,0:T(8,128)}) custom-call(s32[16]{0:T(128)} %left_charge_ref.1, s32[16]{0:T(128)} %right_charge_ref.1, s32[16,2]{1,0:T(8,128)} %copy.9.channel_ref, f32[8,4,4]{2,1,0:T(4,128)} %copy.10.operator_ref, f32[6,256,512]{2,1,0:T(8,128)} %wave_ref.1, bf16[8,16,2,8,128]{4,3,2,1,0:T(8,128)(2,1)} %lt_ref.1, ...), custom_call_target="tpu_custom_call" | custom-call | tf_op jit(solution)/shard_map/whole/pallas_call | solution.py:751
  217.4 0.0 copy-start
  217.4 2.8 %copy.13 = f32[6,16,4096]{2,1,0:T(8,128)} copy(f32[6,16,4096]{2,1,0:T(8,128)} %get-tuple-element.4) | data formatting | bytes 3145728
  220.2 0.0 copy-done
  220.2 1.1 copy.14
Async XLA Ops:
  217.4 2.8 %copy-start = (f32[6,128,512]{2,1,0:T(8,128)S(1)}, f32[6,128,512]{2,1,0:T(8,128)}, u32[]{:S(2)}) copy-start(f32[6,128,512]{2,1,0:T(8,128)} %get-tuple-element.5) | copy-start | bytes 4718596
